TPU v7x, 256 devices: a whole 4x4x8 slice. The times are simulated.
256 devices in a mesh: row: 32 (over y, z), col: 8 (over x, core).
Axes of the slice: x: 4, y: 4, z: 8, core: 2. Of those that a mesh axis runs over, the one named last changes fastest.
Arguments:
- panel_one: bfloat16 [512, 32768], P('col', 'row'), may hold values from -1.1953125 to 1.1953125
- panel_two: bfloat16 [512, 32768], P('col', 'row'), may hold values from -3 to 3
- inverse_one: bfloat16 [512, 512], replicated
- inverse_two: bfloat16 [512, 512], replicated
- column_blocks: int32 [4], replicated, may hold values from 0 to 255, as said below
- row_map: int32 [256], P('row'), may hold values from 0 to 255, as said below
- targets: bfloat16 [32, 8, 128, 128, 128], P('row', 'col'), may hold values from -6 to 6
- rows_one: int32 [32, 8, 128], P('row', 'col'), may hold values from 0 to 255, as said below
- cols_one: int32 [32, 8, 128], P('row', 'col'), may hold values from 0 to 255, as said below
- rows_two: int32 [32, 8, 128], P('row', 'col'), may hold values from 0 to 255, as said below
- cols_two: int32 [32, 8, 128], P('row', 'col'), may hold values from 0 to 255, as said below
Outputs:
- lower_one: bfloat16 [512, 32768], P('col', 'row')
- lower_two: bfloat16 [512, 32768], P('col', 'row')
- trailing: bfloat16 [32, 8, 128, 128, 128], P('row', 'col')
Inputs may be any that keep to these rules, and one draw needn't show every extreme that they name: `column_blocks`: the entries are distinct. row_map[j] // 8 equals j // 8; within each aligned run of 8 entries every value of the run appears once. rows_one[r, c, s] // 8 equals r. cols_one[r, c, s] % 8 equals c. rows_two[r, c, s] // 8 equals r. cols_two[r, c, s] % 8 equals c.
All inputs are finite; a program needn't handle non-finite values.
Results may differ from a plain program's by a relative error of at most 0.006.
Values may be sent and summed in bfloat16 or wider, within the bound.
A program may use at most 192 MiB of HBM per device.

v0:
```python
import jax
import jax.numpy as jnp
from jax import lax
from jax.sharding import PartitionSpec as P


def factor_panel(panel_part, inverse):
    summed = jnp.dot(
        inverse,
        lax.all_gather(panel_part, "col", axis=0, tiled=True),
        preferred_element_type=jnp.float32,
    )
    return summed.astype(jnp.bfloat16)


def bridge_columns(lower_full, column_blocks, slab_rows, block_size):
    local_count = lower_full.shape[1] // block_size
    begin_col = lax.axis_index("col") * slab_rows
    chosen = column_blocks[begin_col // block_size]
    offset = begin_col % block_size
    column_piece = lax.dynamic_slice_in_dim(
        lower_full, chosen % local_count * block_size + offset, slab_rows, 1
    )
    owner_row = chosen // local_count
    owned_here = owner_row == lax.axis_index("row")
    summed = lax.psum(
        jnp.where(owned_here, column_piece.astype(jnp.float32), 0.0).astype(jnp.bfloat16), "row"
    )
    return summed


def pick_tiles(lower_full, block_size):
    col_count = lax.axis_size("col")
    panel_width, row_count = lower_full.shape
    grouped = lower_full.reshape(
        panel_width, row_count // (block_size * col_count), col_count, block_size
    )
    chosen = lax.dynamic_index_in_dim(grouped, lax.axis_index("col"), 2, keepdims=False)
    return chosen.reshape(panel_width, -1)


def gather_tiles(lower_full, block_size):
    return lax.all_gather(pick_tiles(lower_full, block_size), "row", axis=1, tiled=True)


def schur_terms(lower_full, tiles, slot_rows, slot_cols, block_size):
    panel_width = lower_full.shape[0]
    local_blocks = lower_full.reshape(panel_width, -1, block_size)
    column_set = tiles.reshape(panel_width, -1, block_size)
    local_count = local_blocks.shape[1]
    left_tiles = jnp.take(local_blocks, slot_rows.reshape(-1) % local_count, axis=1)
    right_tiles = jnp.take(column_set, slot_cols.reshape(-1) // lax.axis_size("col"), axis=1)
    return jnp.einsum("wsx,wsy->sxy", left_tiles, right_tiles, preferred_element_type=jnp.float32)


def own_slice(lower_full, slab_rows):
    return lax.dynamic_slice_in_dim(lower_full, lax.axis_index("col") * slab_rows, slab_rows, 0)


def per_device(
    panel_one,
    panel_two,
    inverse_one,
    inverse_two,
    column_blocks,
    row_map,
    targets,
    rows_one,
    cols_one,
    rows_two,
    cols_two,
):
    block_size = targets.shape[-1]
    slab_rows = panel_one.shape[0]
    panel_width = inverse_one.shape[0]
    row_count = panel_one.shape[1]
    local_count = row_count // block_size
    lower_one = factor_panel(panel_one, inverse_one)
    blocks_one = lower_one.reshape(panel_width, local_count, block_size)
    bridge = bridge_columns(lower_one, column_blocks, slab_rows, block_size)
    mapped = jnp.take(blocks_one, row_map % local_count, axis=1).reshape(panel_width, row_count)
    update = lax.dot_general(
        bridge, mapped, (((0,), (0,)), ((), ())), preferred_element_type=jnp.float32
    )
    updated = (panel_two.astype(jnp.float32) - update).astype(jnp.bfloat16)
    lower_two = factor_panel(updated, inverse_two)
    tiles_one = gather_tiles(lower_one, block_size)
    tiles_two = gather_tiles(lower_two, block_size)
    terms = schur_terms(lower_one, tiles_one, rows_one, cols_one, block_size)
    terms = terms + schur_terms(lower_two, tiles_two, rows_two, cols_two, block_size)
    trailing = (
        (targets.astype(jnp.float32).reshape(terms.shape) - terms)
        .astype(jnp.bfloat16)
        .reshape(targets.shape)
    )
    return (own_slice(lower_one, slab_rows), own_slice(lower_two, slab_rows), trailing)


def solution(mesh):
    return jax.shard_map(
        per_device,
        mesh=mesh,
        in_specs=(
            P("col", "row"),
            P("col", "row"),
            P(),
            P(),
            P(),
            P("row"),
            P("row", "col", None, None, None),
            P("row", "col", None),
            P("row", "col", None),
            P("row", "col", None),
            P("row", "col", None),
        ),
        out_specs=(P("col", "row"), P("col", "row"), P("row", "col", None, None, None)),
        check_vma=False,
    )
```

profile of v0, /device:TPU:2, one launch (start us, length us, event | category | flops | bytes accessed | tf_op | source)
XLA Modules:
  0.0 418.5 jit_solution(15414585895211025504)
XLA Ops:
  7.3 0.7 all-gather.7.cloned.1.call-update
  8.0 1.2 dynamic_slice.20
  11.9 0.7 compare_and_fusion.4
  12.6 0.1 broadcast_bitcast_fusion
  12.7 24.4 %all-gather.7.cloned.1.call-done = bf16[512,1024]{1,0:T(8,128)(2,1)} async-done(((bf16[64,1024]{1,0:T(8,128)(2,1)}), bf16[512,1024]{1,0:T(8,128)(2,1)}) %all-gather.7.cloned.1.call-update) | async-done | bytes 1048592 | tf_op jit(solution)/shard_map/all_gather | solution.py:10
  37.1 1.9 convolution_convert_fusion.1
  39.0 0.2 copy_bitcast_fusion
  39.2 0.8 select_convert_fusion
  40.1 1.7 gather_fusion
  41.7 2.3 copy.22
  44.0 2.4 bitcast_select_fusion
  46.4 138.7 %all-reduce.2.cloned.1.call-done = bf16[512,64]{1,0:T(8,128)(2,1)} async-done(((bf16[512,64]{1,0:T(8,128)(2,1)}), bf16[512,64]{1,0:T(8,128)(2,1)}) %all-reduce.2.cloned.1.call-update) | async-done | bytes 65552 | tf_op jit(solution)/shard_map/psum | solution.py:26
  185.1 2.4 fusion.23
  187.5 1.3 copy.30
  188.9 1.6 constant_dynamic-slice_fusion.1
  190.5 0.2 all-gather.13.cloned.1.call-start
  190.7 19.4 %all-gather.9.cloned.1.call-done = bf16[512,1024]{1,0:T(8,128)(2,1)} async-done(((bf16[64,1024]{1,0:T(8,128)(2,1)}), bf16[512,1024]{1,0:T(8,128)(2,1)}) %all-gather.9.cloned.1.call-update) | async-done | bytes 1048592 | tf_op jit(solution)/shard_map/all_gather | solution.py:10
  210.1 2.1 convolution_convert_fusion
  212.2 0.7 constant_dynamic-slice_fusion
  213.1 8.3 %gather_fusion.1 = bf16[128,512,128]{2,1,0:T(8,128)(2,1)} fusion(bf16[512,8,128]{2,0,1:T(8,128)(2,1)S(1)} %copy_bitcast_fusion, s32[1024]{0:T(1024)S(1)} %pad_clamp_fusion.3), kind=kCustom, calls=%fused_computation.clone | custom fusion | bytes 33554944 | tf_op jit(solution)/shard_map/jit(_take)/gather | solution.py:51
  221.4 1.6 constant_dynamic-slice_fusion.2
  222.9 0.1 dynamic-slice_bitcast_fusion
  223.1 0.8 copy.28
  223.8 8.2 %gather_fusion.3 = bf16[128,512,128]{1,2,0:T(8,128)(2,1)} fusion(bf16[512,8,128]{0,2,1:T(8,128)(2,1)S(1)} %bitcast.77, s32[1024]{0:T(1024)S(1)} %pad_clamp_fusion.1), kind=kCustom, calls=%fused_computation.2.clone | custom fusion | bytes 33554944 | tf_op jit(solution)/shard_map/jit(_take)/gather | solution.py:51
  232.0 63.8 %all-gather.11.cloned.1.call-done = bf16[512,1,1,4096]{0,3,2,1:T(8,128)(2,1)} async-done(((bf16[512,1,1,128]{0,3,2,1:T(8,128)(2,1)}), bf16[512,1,1,4096]{0,3,2,1:T(8,128)(2,1)}) %all-gather.11.cloned.1.call-update) | async-done | bytes 4194320 | tf_op jit(solution)/shard_map/all_gather | solution.py:43
  295.9 6.4 %copy.25 = bf16[512,32,128]{2,0,1:T(8,128)(2,1)} copy(bf16[512,32,128]{0,2,1:T(8,128)(2,1)} %bitcast.79) | data formatting | bytes 8388608 | tf_op jit(solution)/shard_map/reshape | solution.py:49
  302.3 10.6 %gather_fusion.2 = bf16[128,512,128]{2,1,0:T(8,128)(2,1)} fusion(bf16[512,32,128]{2,0,1:T(8,128)(2,1)} %copy.25, s32[1024]{0:T(1024)S(1)} %pad_clamp_fusion.2), kind=kCustom, calls=%fused_computation.1.clone | custom fusion | bytes 33554944 | tf_op jit(solution)/shard_map/jit(_take)/gather | solution.py:52
  312.9 16.8 %fusion.3 = f32[128,128,128]{2,1,0:T(8,128)} fusion(bf16[128,512,128]{2,1,0:T(8,128)(2,1)} %gather_fusion.2, bf16[128,512,128]{2,1,0:T(8,128)(2,1)} %gather_fusion.1, pred[128]{0:T(512)(128)(4,1)S(1)} %get-tuple-element.20, pred[128]{0:T(512)(128)(4,1)S(1)} %get-tuple-element.26), kind=kOutput, calls=%fused_computation.8 | convolution fusion | flops 2164260864 | bytes 41943296 | tf_op jit(solution)/shard_map/wsx,wsy->sxy/dot_general | solution.py:53
  329.7 47.2 %all-gather.13.cloned.1.call-done = bf16[512,1,1,4096]{0,3,2,1:T(8,128)(2,1)} async-done(((bf16[512,1,1,128]{0,3,2,1:T(8,128)(2,1)}), bf16[512,1,1,4096]{0,3,2,1:T(8,128)(2,1)}) %all-gather.13.cloned.1.call-update) | async-done | bytes 4194320 | tf_op jit(solution)/shard_map/all_gather | solution.py:43
  376.9 6.4 %copy.27 = bf16[512,32,128]{2,0,1:T(8,128)(2,1)} copy(bf16[512,32,128]{0,2,1:T(8,128)(2,1)} %bitcast.80) | data formatting | bytes 8388608 | tf_op jit(solution)/shard_map/reshape | solution.py:49
  383.3 10.5 %gather_fusion.4 = bf16[128,512,128]{2,1,0:T(8,128)(2,1)} fusion(bf16[512,32,128]{2,0,1:T(8,128)(2,1)} %copy.27, s32[1024]{0:T(1024)S(1)} %pad_clamp_fusion), kind=kCustom, calls=%fused_computation.3.clone | custom fusion | bytes 33554944 | tf_op jit(solution)/shard_map/jit(_take)/gather | solution.py:52
  393.8 18.2 %fusion.18 = bf16[1,1,128,128,128]{4,3,2,1,0:T(8,128)(2,1)} fusion(f32[128,128,128]{2,1,0:T(8,128)} %fusion.3, bf16[1,1,128,128,128]{4,3,2,1,0:T(8,128)(2,1)} %param.21, bf16[128,512,128]{2,1,0:T(8,128)(2,1)} %gather_fusion.4, pred[128]{0:T(512)(128)(4,1)S(1)} %get-tuple-element.16, bf16[128,512,128]{1,2,0:T(8,128)(2,1)} %gather_fusion.3, ...), kind=kOutput, calls=%fused_computation.24 | convolution fusion | flops 2172649472 | bytes 50331904 | tf_op jit(solution)/shard_map/wsx,wsy->sxy/dot_general | solution.py:53
  (29 shorter events, 0.3 us)
Async XLA Ops:
  7.2 29.9 %copy-start = (bf16[512,512]{1,0:T(8,128)(2,1)S(1)}, bf16[512,512]{1,0:T(8,128)(2,1)}, u32[]{:S(2)}) copy-start(bf16[512,512]{1,0:T(8,128)(2,1)} %param.17) | copy-start | bytes 1572868
  7.2 205.8 %copy-start.3 = (s32[1,1,128]{2,1,0:T(1,128)S(1)}, s32[1,1,128]{2,1,0:T(1,128)}, u32[]{:S(2)}) copy-start(s32[1,1,128]{2,1,0:T(1,128)} %param.23) | copy-start | bytes 1540
  7.2 205.8 %copy-start.4 = (s32[1,1,128]{2,1,0:T(1,128)S(1)}, s32[1,1,128]{2,1,0:T(1,128)}, u32[]{:S(2)}) copy-start(s32[1,1,128]{2,1,0:T(1,128)} %param.22) | copy-start | bytes 1540
  7.2 205.8 %copy-start.5 = (s32[1,1,128]{2,1,0:T(1,128)S(1)}, s32[1,1,128]{2,1,0:T(1,128)}, u32[]{:S(2)}) copy-start(s32[1,1,128]{2,1,0:T(1,128)} %param.25) | copy-start | bytes 1540
  7.2 205.8 %copy-start.6 = (s32[1,1,128]{2,1,0:T(1,128)S(1)}, s32[1,1,128]{2,1,0:T(1,128)}, u32[]{:S(2)}) copy-start(s32[1,1,128]{2,1,0:T(1,128)} %param.24) | copy-start | bytes 1540
  7.2 29.8 %all-gather.7.cloned.1.call-start = ((), (), s32[]{:S(2)}) async-start(), calls=%async_computation | async-start | bytes 1179648 | tf_op jit(solution)/shard_map/all_gather | solution.py:10
  8.0 177.1 %all-reduce.2.cloned.1.call-start = ((), (), s32[]{:S(2)}) async-start(), calls=%async_computation.1 | async-start | bytes 262144 | tf_op jit(solution)/shard_map/psum | solution.py:26
  39.0 151.7 %copy-start.2 = (bf16[512,1024]{1,0:T(8,128)(2,1)}, bf16[512,1024]{1,0:T(8,128)(2,1)S(1)}, u32[]{:S(2)}) copy-start(bf16[512,1024]{1,0:T(8,128)(2,1)S(1)} %convolution_convert_fusion.1) | copy-start | bytes 3145732
  40.0 170.1 %all-gather.9.cloned.1.call-start = ((), (), s32[]{:S(2)}) async-start(), calls=%async_computation.2 | async-start | bytes 1179648 | tf_op jit(solution)/shard_map/all_gather | solution.py:10
  187.5 108.4 %all-gather.11.cloned.1.call-start = ((), (), s32[]{:S(2)}) async-start(), calls=%async_computation.3 | async-start | bytes 4325376 | tf_op jit(solution)/shard_map/all_gather | solution.py:43
  190.5 186.4 %all-gather.13.cloned.1.call-start = ((), (), s32[]{:S(2)}) async-start(), calls=%async_computation.4 | async-start | bytes 4325376 | tf_op jit(solution)/shard_map/all_gather | solution.py:43
  393.8 18.2 %copy-start.1 = (bf16[512,512]{1,0:T(8,128)(2,1)S(1)}, bf16[512,512]{1,0:T(8,128)(2,1)}, u32[]{:S(2)}) copy-start(bf16[512,512]{1,0:T(8,128)(2,1)} %param.17) | copy-start | bytes 1572868
Sparse Core Ops, SparseCore 0:
  9.9 27.1 all-gather.6
  41.1 143.9 all-reduce.1
  187.6 22.4 all-gather.8
  212.6 83.2 all-gather.10
  298.3 78.5 all-gather.12
where the time goes:
time: 419 us
  waiting for transfers between devices  294 us (70%)
  local copies, waits for them, and re-layouts  61.9 us (15%)
  matrix products  41.4 us (10%)
  between operations  16.6 us (4%)
    psum x1, waiting for transfers between devices, bridge_columns(): lax.psum(jnp.where(owned_here, column_piece.astype(jnp.float32), 0.0).ast...  139 us
    all_gather x2, waiting for transfers between devices, gather_tiles(): lax.all_gather(pick_tiles(lower_full, block_size), 'row', axis=1, tiled=T...  111 us
    all_gather x2, waiting for transfers between devices, factor_panel(): lax.all_gather(panel_part, 'col', axis=0, tiled=True)  43.8 us
    dot_general x2, matrix products, schur_terms(): jnp.einsum('wsx,wsy->sxy', left_tiles, right_tiles, preferred_element_typ...  35 us
    gather x2, local copies, waits for them, and re-layouts, schur_terms(): jnp.take(column_set, slot_cols.reshape(-1) // lax.axis_size('col'), axis=1)  21.1 us
    gather x2, local copies, waits for them, and re-layouts, schur_terms(): jnp.take(local_blocks, slot_rows.reshape(-1) % local_count, axis=1)  16.5 us
    reshape x2, local copies, waits for them, and re-layouts, schur_terms(): column_set = tiles.reshape(panel_width, -1, block_size)  12.8 us
  transfers between devices with their start and end apart: 5, of which 5 were waited for; matrix products, arithmetic and copies ran while one was open for 16% of the time, Pallas kernels for 0%

commit v1 on v0

v1 whole, which is shorter than its diff:
```python
import functools
import heapq

import jax
import jax.numpy as jnp
from jax import lax
from jax.experimental import pallas as pl
from jax.experimental.pallas import tpu as pltpu
from jax.sharding import PartitionSpec as P

MESH = pl.DeviceIdType.MESH
NY, NZ, NX, NC = 4, 8, 4, 2

PART_A, HALF_A0, HALF_A1 = (0, 304), (0, 160), (160, 144)
PART_B, HALF_B0, HALF_B1 = (304, 208), (304, 112), (416, 96)
STEP = {"y+": (1, 0), "y-": (-1, 0), "z+": (0, 1), "z-": (0, -1)}
OWN_SENDS = (
    ("z+", PART_A),
    ("z-", PART_A),
    ("y+", PART_B),
    ("y-", PART_B),
    ("y+", PART_A),
    ("y-", PART_A),
    ("z+", PART_B),
    ("z-", PART_B),
)


def wrapped(value, size):
    value %= size
    return value - size if value > size // 2 else value


def next_source(source, way):
    dy, dz = STEP[way]
    return (wrapped(source[0] - dy, NY), wrapped(source[1] - dz, NZ))


def forwards(way, piece, source, seen):
    sy, sz = source
    if piece[0] < PART_A[1]:
        first, second = HALF_A0, HALF_A1
        if way[0] == "z":
            half = first if way == "z+" else second
            out = [(way, PART_A)] if abs(sz) < 3 else []
            if abs(sz) == 3:
                out.append((way, half))
            if abs(sz) < 4 or {first, second} <= seen:
                out += [("y+", PART_A), ("y-", PART_A)]
            return out
        return [(way, first if way == "y+" else second)] if abs(sy) == 1 else []
    first, second = HALF_B0, HALF_B1
    if way[0] == "y":
        out = []
        if abs(sy) == 1:
            out.append((way, first if way == "y+" else second))
        if abs(sy) == 1 or {first, second} <= seen:
            out += [("z+", PART_B), ("z-", PART_B)]
        return out
    if abs(sz) < 3:
        return [(way, PART_B)]
    return [(way, first if way == "z+" else second)] if abs(sz) == 3 else []


def gather_plan(rate=47.0, latency=1.7):
    free = dict.fromkeys(STEP, 0.0)
    seen, heap, plan = {}, [], []

    def send(now, way, piece, source):
        free[way] = max(now, free[way]) + piece[1] * 256 / 1000 / rate
        heapq.heappush(
            heap, (free[way] + latency, len(heap) + len(plan), way, piece, next_source(source, way))
        )

    for way, piece in OWN_SENDS:
        send(0.0, way, piece, (0, 0))
    while heap:
        now, _, way, piece, source = heapq.heappop(heap)
        seen.setdefault(source, set()).add(piece)
        out = forwards(way, piece, source, seen[source])
        plan.append((now, way, piece, source, out))
        for onward, part in out:
            send(now, onward, part, source)
    return plan


PLAN = gather_plan()
EVENT = {(way, piece, source): i for i, (_, way, piece, source, _) in enumerate(PLAN)}
N_EVENTS = len(PLAN)


def tile_order():
    rows, done = {}, []
    for now, _, piece, source, _ in PLAN:
        rows[source] = rows.get(source, 0) + piece[1]
        if rows[source] == 512:
            done.append((now, source))
    return [(0.0, (0, 0))] + done


def kernel(
    panel_one,
    panel_two,
    inverse_one,
    inverse_two,
    targets,
    column_blocks,
    row_map,
    rows_one,
    cols_one,
    rows_two,
    cols_two,
    lower_one,
    lower_two,
    trailing,
    slab_one,
    slab_two,
    full_one,
    full_two,
    inv_one,
    inv_two,
    own_raw,
    pick,
    ring_z,
    mid,
    ring_y,
    raw_bridge,
    bridge_t,
    blocks_one,
    blocks_two,
    left_one,
    left_two,
    tiles,
    products,
    partial,
    staged,
    local_sem,
    out_sem,
    x_send,
    x_recv,
    side_recv,
    swap_send,
    swap_recv,
    sum_send,
    sum_recv,
    tile_send,
    tile_recv,
):
    f32, bf16 = jnp.float32, jnp.bfloat16
    row, col = lax.axis_index("row"), lax.axis_index("col")
    y, z = row // NZ, row % NZ
    x, core = col // NC, col % NC
    slab = slab_one.shape[1]
    base = pl.multiple_of(col * slab, slab)

    def row_at(dy, dz):
        return ((y + dy + NY) % NY) * NZ + (z + dz + NZ) % NZ

    def col_at(dx):
        return ((x + dx) % NX) * NC + core

    partner = x * NC + (1 - core)

    def remote(src, dst, send, recv, device):
        return pltpu.make_async_remote_copy(
            src_ref=src, dst_ref=dst, send_sem=send, recv_sem=recv, device_id=device, device_id_type=MESH
        )

    def await_recv(ref, sem):
        remote(ref, ref, tile_send.at[0], sem, (row, partner)).wait_recv()

    def await_send(ref, sem):
        remote(ref, ref, sem, tile_recv.at[0, 0], (row, partner)).wait_send()

    loads = []
    n_blocks = slab_one.shape[0]
    for which, (panel, mine) in enumerate(((panel_one, slab_one), (panel_two, slab_two))):
        for j in range(n_blocks):
            loads.append(pltpu.make_async_copy(panel.at[:, pl.ds(j * 128, 128)], mine.at[j], local_sem.at[which]))
    for copy in loads:
        copy.start()
    load_inv_one = pltpu.make_async_copy(inverse_one, inv_one, local_sem.at[2])
    load_inv_two = pltpu.make_async_copy(inverse_two, inv_two, local_sem.at[3])
    load_targets = pltpu.make_async_copy(targets, staged, local_sem.at[4])
    load_inv_one.start()
    load_inv_two.start()
    load_targets.start()

    barrier = pltpu.get_barrier_semaphore()
    in_row = [(row, (col + d) % (NX * NC)) for d in range(1, NX * NC)]
    along_z = [(row_at(0, d), col) for d in range(1, NZ)]
    along_y = [(row_at(d, 0), col) for d in range(1, NY)]
    for device in in_row + along_z + along_y:
        pl.semaphore_signal(barrier, inc=1, device_id=device, device_id_type=MESH)
    pltpu.make_async_copy(slab_one, slab_one, local_sem.at[0]).wait()
    pltpu.make_async_copy(slab_two, slab_two, local_sem.at[1]).wait()
    keep_one = pltpu.make_async_copy(slab_one, full_one.at[:, pl.ds(base, slab), :], local_sem.at[5])
    keep_two = pltpu.make_async_copy(slab_two, full_two.at[:, pl.ds(base, slab), :], local_sem.at[6])
    keep_raw = pltpu.make_async_copy(slab_one.at[col], own_raw.at[pl.ds(base, slab), :], local_sem.at[7])
    keep_one.start()
    keep_two.start()
    keep_raw.start()
    pl.semaphore_wait(barrier, len(in_row) + len(along_z) + len(along_y))

    for _, peer in in_row:
        remote(
            slab_one.at[peer], own_raw.at[pl.ds(base, slab), :], swap_send, swap_recv, (row, peer)
        ).start()

    for k in range(4):
        chosen = column_blocks[k]
        block = slab_one[chosen % n_blocks]
        block = jnp.where(chosen // n_blocks == row, block.astype(f32), 0.0).astype(bf16)
        pick[2 * k] = block[:32]
        pick[2 * k + 1] = block[32:]

    def spread(mine, full, which):
        for dx in range(1, NX):
            remote(
                mine, full.at[:, pl.ds(base, slab), :], x_send.at[which], x_recv.at[which, dx - 1], (row, col_at(dx))
            ).start()
        remote(
            mine, full.at[:, pl.ds(base, slab), :], x_send.at[which], side_recv.at[which], (row, partner)
        ).start()

    def pass_on(full, which, dx):
        ref = full.at[:, pl.ds(pl.multiple_of(col_at(NX - dx) * slab, slab), slab), :]
        await_recv(ref, x_recv.at[which, dx - 1])
        remote(ref, ref, x_send.at[which], side_recv.at[which], (row, partner)).start()

    def side_wait(full, which):
        await_recv(full.at[:, pl.ds(0, NX * slab), :], side_recv.at[which])

    def sum_z_send():
        for d in range(1, NZ):
            remote(
                pick.at[(z + d) % NZ], ring_z.at[d - 1], sum_send.at[0], sum_recv.at[0], (row_at(0, d), col)
            ).start()

    piece_k = z // 2
    piece_rows = pl.ds(pl.multiple_of(base + 32 * (z % 2), 32), 32)

    def sum_y_send():
        await_recv(ring_z, sum_recv.at[0])
        total = pick[z].astype(f32)
        for d in range(NZ - 1):
            total += ring_z[d].astype(f32)
        mid[...] = total.astype(bf16)
        for d in range(1, NY):
            remote(mid, ring_y.at[d - 1], sum_send.at[1], sum_recv.at[1], (row_at(d, 0), col)).start()

    def sum_z_return():
        await_recv(ring_y, sum_recv.at[1])
        total = mid[...].astype(f32)
        for d in range(NY - 1):
            total += ring_y[d].astype(f32)
        raw_bridge[piece_k, piece_rows, :] = total.astype(bf16)
        ref = raw_bridge.at[piece_k, piece_rows, :]
        for d in range(1, NZ):
            remote(ref, ref, sum_send.at[2], sum_recv.at[2], (row_at(0, d), col)).start()

    def bridge_spread():
        await_recv(ring_z, sum_recv.at[2])
        spread(raw_bridge.at[:, pl.ds(base, slab), :], raw_bridge, 2)

    def tile_copy(p, way, piece, source):
        ref = tiles.at[p, row_at(*source), pl.ds(*piece), :]
        event = EVENT[(way, piece, next_source(source, way))]
        remote(ref, ref, tile_send.at[p], tile_recv.at[p, event], (row_at(*STEP[way]), col)).start()

    def own_sends(p):
        for way, piece in OWN_SENDS:
            tile_copy(p, way, piece, (0, 0))

    def tile_event(p, index):
        _, _, piece, source, out = PLAN[index]
        await_recv(tiles.at[p, row_at(*source), pl.ds(*piece), :], tile_recv.at[p, index])
        for way, part in out:
            tile_copy(p, way, part, source)

    def dot(a, b):
        return jnp.dot(a, b, preferred_element_type=f32)

    def first_block():
        await_recv(own_raw.at[pl.ds(0, (NX * NC - 1) * slab), :], swap_recv)
        tiles[0, row] = dot(inv_one[...], own_raw[...]).astype(bf16)

    def store_pair(blocks, left, i, value):
        for h in range(2):
            part = value[:, h * 128 : (h + 1) * 128]
            blocks[2 * i + h] = part.astype(bf16)
            left[pl.ds(pl.multiple_of((2 * i + h) * 128, 128), 128), :] = part.T.astype(bf16)

    def factor_one():
        @pl.loop(0, n_blocks // 2)
        def _(i):
            pair = jnp.concatenate([full_one[2 * i], full_one[2 * i + 1]], axis=1)
            store_pair(blocks_one, left_one, i, dot(inv_one[...], pair))

    def bridge_build():
        @pl.loop(0, 4)
        def _(k):
            value = dot(inv_one[...], raw_bridge[k])
            bridge_t[pl.ds(pl.multiple_of(k * 128, 128), 128), :] = value.T.astype(bf16)

    def pair_two(i):
        mapped = jnp.concatenate(
            [blocks_one[row_map[2 * i] % n_blocks], blocks_one[row_map[2 * i + 1] % n_blocks]], axis=1
        )
        pair = jnp.concatenate([full_two[2 * i], full_two[2 * i + 1]], axis=1)
        updated = (pair.astype(f32) - dot(bridge_t[...], mapped)).astype(bf16)
        store_pair(blocks_two, left_two, i, dot(inv_two[...], updated))

    def factor_two_own():
        pair_two(col // 2)
        tiles[1, row] = blocks_two[col]

    def factor_two_rest():
        @pl.loop(1, n_blocks // 2)
        def _(i):
            pair_two((col // 2 + i) % (n_blocks // 2))

    def products_of(p, left, first, second):
        t0, t1 = row_at(*first), row_at(*second)

        @pl.loop(0, 2)
        def _(m):
            pair = jnp.concatenate([tiles[p, t0], tiles[p, t1]], axis=1)
            value = dot(left[pl.ds(pl.multiple_of(m * 512, 512), 512), :], pair)
            for h, t in enumerate((t0, t1)):
                products[pl.ds(t * n_blocks + 4 * m, 4)] = value[:, h * 128 : (h + 1) * 128].reshape(4, 128, 128)

    n_slots = staged.shape[0]

    def combine_one():
        load_targets.wait()

        @pl.loop(0, n_slots)
        def _(s):
            index = (cols_one[s] // n_blocks) * n_blocks + rows_one[s] % n_blocks
            partial[s] = staged[s].astype(f32) - products[index]

    group = 16

    def result_copy(g):
        return pltpu.make_async_copy(
            staged.at[pl.ds(g * group, group)], trailing.at[pl.ds(g * group, group)], out_sem.at[g]
        )

    def combine_two():
        for g in range(n_slots // group):

            @pl.loop(g * group, (g + 1) * group)
            def _(s):
                index = (cols_two[s] // n_blocks) * n_blocks + rows_two[s] % n_blocks
                staged[s] = (partial[s] - products[index]).astype(bf16)

            result_copy(g).start()

    def write_lower(blocks, out, which):
        return [
            pltpu.make_async_copy(
                blocks.at[j, pl.ds(base, slab), :], out.at[:, pl.ds(j * 128, 128)], local_sem.at[8 + which]
            )
            for j in range(n_blocks)
        ]

    def start_all(copies):
        for copy in copies:
            copy.start()

    lower_copies = write_lower(blocks_one, lower_one, 0) + write_lower(blocks_two, lower_two, 1)

    sum_z_send()
    spread(slab_one, full_one, 0)
    spread(slab_two, full_two, 1)
    load_inv_one.wait()
    load_inv_two.wait()
    keep_raw.wait()
    keep_one.wait()
    keep_two.wait()
    first_block()
    own_sends(0)

    one, two = 0.0, 18.5
    work = [
        (0.6, sum_y_send),
        (3.6, sum_z_return),
        (4.0, lambda: pass_on(full_one, 0, 1)),
        (4.1, lambda: pass_on(full_one, 0, 3)),
        (4.9, lambda: pass_on(full_one, 0, 2)),
        (6.5, lambda: side_wait(full_one, 0)),
        (6.6, factor_one),
        (6.7, lambda: start_all(lower_copies[:n_blocks])),
        (8.6, bridge_spread),
        (9.0, lambda: pass_on(full_two, 1, 1)),
        (9.1, lambda: pass_on(full_two, 1, 3)),
        (10.6, lambda: pass_on(full_two, 1, 2)),
        (12.2, lambda: side_wait(full_two, 1)),
        (13.8, lambda: pass_on(raw_bridge, 2, 1)),
        (13.9, lambda: pass_on(raw_bridge, 2, 3)),
        (14.8, lambda: pass_on(raw_bridge, 2, 2)),
        (16.3, lambda: side_wait(raw_bridge, 2)),
        (16.4, bridge_build),
        (16.5, factor_two_own),
        (16.6, lambda: own_sends(1)),
        (16.7, factor_two_rest),
        (16.8, lambda: start_all(lower_copies[n_blocks:])),
    ]
    for i, (now, *_) in enumerate(PLAN):
        work.append((one + now, functools.partial(tile_event, 0, i)))
        work.append((two + now, functools.partial(tile_event, 1, i)))
    order = tile_order()
    for i in range(0, len(order), 2):
        now, pair = order[i + 1][0], (order[i][1], order[i + 1][1])
        work.append((max(one + now, 6.61) + 0.01, functools.partial(products_of, 0, left_one, *pair)))
        work.append((max(two + now, one + PLAN[-1][0] + 0.1) + 0.01, functools.partial(products_of, 1, left_two, *pair)))
    work.append((one + PLAN[-1][0] + 0.1, combine_one))
    for _, step in sorted(work, key=lambda item: item[0]):
        step()
    combine_two()

    for g in range(n_slots // group):
        result_copy(g).wait()
    pltpu.make_async_copy(lower_one, lower_one, local_sem.at[8]).wait()
    pltpu.make_async_copy(lower_two, lower_two, local_sem.at[9]).wait()
    await_send(own_raw.at[pl.ds(0, (NX * NC - 1) * slab), :], swap_send)
    await_send(ring_z, sum_send.at[0])
    await_send(ring_y, sum_send.at[1])
    await_send(ring_z, sum_send.at[2])
    await_send(full_one.at[pl.ds(0, n_blocks - 1)], x_send.at[0])
    await_send(full_two.at[pl.ds(0, n_blocks - 1)], x_send.at[1])
    await_send(full_two.at[pl.ds(0, n_blocks - 1), pl.ds(0, 256), :], x_send.at[2])
    await_send(tiles.at[0, pl.ds(0, NY * NZ - 1)], tile_send.at[0])
    await_send(tiles.at[1, pl.ds(0, NY * NZ - 1)], tile_send.at[1])


def per_device(
    panel_one,
    panel_two,
    inverse_one,
    inverse_two,
    column_blocks,
    row_map,
    targets,
    rows_one,
    cols_one,
    rows_two,
    cols_two,
):
    slab, row_count = panel_one.shape
    width = inverse_one.shape[0]
    size = targets.shape[-1]
    n_slots = targets.shape[2]
    n_blocks = row_count // size
    n_rows = NY * NZ
    bf16, f32 = jnp.bfloat16, jnp.float32
    vmem = pltpu.VMEM
    dma = pltpu.SemaphoreType.DMA
    in_hbm = pl.BlockSpec(memory_space=pl.ANY)
    in_smem = pl.BlockSpec(memory_space=pltpu.SMEM)
    lower_one, lower_two, trailing = pl.pallas_call(
        kernel,
        out_shape=(
            jax.ShapeDtypeStruct(panel_one.shape, bf16),
            jax.ShapeDtypeStruct(panel_two.shape, bf16),
            jax.ShapeDtypeStruct((n_slots, size, size), bf16),
        ),
        in_specs=[in_hbm] * 5 + [in_smem] * 6,
        out_specs=(in_hbm,) * 3,
        scratch_shapes=[
            vmem((n_blocks, slab, size), bf16),
            vmem((n_blocks, slab, size), bf16),
            vmem((n_blocks, width, size), bf16),
            vmem((n_blocks, width, size), bf16),
            vmem((width, width), bf16),
            vmem((width, width), bf16),
            vmem((width, size), bf16),
            vmem((8, 32, size), bf16),
            vmem((NZ - 1, 32, size), bf16),
            vmem((32, size), bf16),
            vmem((NY - 1, 32, size), bf16),
            vmem((4, width, size), bf16),
            vmem((width, width), bf16),
            vmem((n_blocks, width, size), bf16),
            vmem((n_blocks, width, size), bf16),
            vmem((row_count, width), bf16),
            vmem((row_count, width), bf16),
            vmem((2, n_rows, width, size), bf16),
            vmem((n_rows * n_blocks, size, size), f32),
            vmem((n_slots, size, size), f32),
            vmem((n_slots, size, size), bf16),
            dma((10,)),
            dma((8,)),
            dma((3,)),
            dma((3, NX - 1)),
            dma((3,)),
            dma,
            dma,
            dma((3,)),
            dma((3,)),
            dma((2,)),
            dma((2, N_EVENTS)),
        ],
        compiler_params=pltpu.CompilerParams(
            collective_id=0, has_side_effects=True, vmem_limit_bytes=62 * 1024 * 1024
        ),
    )(
        panel_one,
        panel_two,
        inverse_one,
        inverse_two,
        targets.reshape(n_slots, size, size),
        column_blocks,
        row_map,
        rows_one.reshape(-1),
        cols_one.reshape(-1),
        rows_two.reshape(-1),
        cols_two.reshape(-1),
    )
    return lower_one, lower_two, trailing.reshape(targets.shape)


def solution(mesh):
    return jax.shard_map(
        per_device,
        mesh=mesh,
        in_specs=(
            P("col", "row"),
            P("col", "row"),
            P(),
            P(),
            P(),
            P("row"),
            P("row", "col", None, None, None),
            P("row", "col", None),
            P("row", "col", None),
            P("row", "col", None),
            P("row", "col", None),
        ),
        out_specs=(P("col", "row"), P("col", "row"), P("row", "col", None, None, None)),
        check_vma=False,
    )
```

time: 419 us -> 97 us (0.23)
  waiting for transfers between devices: 294 us -> 0 us
  Pallas kernels: 0 us -> 86.7 us
  local copies, waits for them, and re-layouts: 61.9 us -> 7.92 us
  matrix products: 41.4 us -> 0 us
  between operations: 16.6 us -> 0.64 us
    all_gather x4 -> x0, waiting for transfers between devices: 155 us -> none  [the longest x2 111 us: gather_tiles(): lax.all_gather(pick_tiles(lower_full, block_size), 'row', axis=1, tiled=T...]
    psum x1 -> x0, waiting for transfers between devices: 139 us -> none  [bridge_columns(): lax.psum(jnp.where(owned_here, column_piece.astype(jnp.float32), 0.0).ast...]
    pallas_call x0 -> x1, Pallas kernels: none -> 86.7 us  [per_device(): pl.pallas_call(kernel, out_shape=(jax.ShapeDtypeStruct(panel_one.shape, b...]
    gather x6 -> x0, local copies, waits for them, and re-layouts: 41.5 us -> none  [the longest x2 21.1 us: schur_terms(): jnp.take(column_set, slot_cols.reshape(-1) // lax.axis_size('col'), axis=1)]
    dot_general x5 -> x0, matrix products: 41.4 us -> none  [the longest x2 35 us: schur_terms(): jnp.einsum('wsx,wsy->sxy', left_tiles, right_tiles, preferred_element_typ...]
    reshape x4 -> x0, local copies, waits for them, and re-layouts: 14.3 us -> none  [the longest x2 12.8 us: schur_terms(): column_set = tiles.reshape(panel_width, -1, block_size)]
    unnamed x15 -> x3, local copies, waits for them, and re-layouts: 0.82 us -> 7.92 us
    dynamic_slice x5 -> x0, local copies, waits for them, and re-layouts: 5.17 us -> none  [the longest x2 2.23 us: pick_tiles(): lax.dynamic_index_in_dim(grouped, lax.axis_index('col'), 2, keepdims=False)]
  transfers between devices with their start and end apart: 5 -> 0, of which waited for: 5 -> 0; matrix products, arithmetic and copies ran while one was open for 16% -> 0% of each run, Pallas kernels for 0% -> 0%
where the time goes in v1:
time: 97 us; the launch traced here: 95.2 us
  Pallas kernels  86.7 us (89%)
  local copies, waits for them, and re-layouts  7.92 us (8%)
    pallas_call x1, Pallas kernels, per_device(): pl.pallas_call(kernel, out_shape=(jax.ShapeDtypeStruct(panel_one.shape, b...  86.7 us
    unnamed x3, local copies, waits for them, and re-layouts  7.92 us

profile of v1, /device:TPU:2, one launch (start us, length us, event | category | flops | bytes accessed | tf_op | source)
XLA Modules:
  0.0 95.2 jit_solution(11608069149743912908)
XLA Ops:
  0.6 86.7 %shard_map.130 = (bf16[64,1024]{1,0:T(8,128)(2,1)}, bf16[64,1024]{1,0:T(8,128)(2,1)}, bf16[128,128,128]{2,1,0:T(8,128)(2,1)}) custom-call(bf16[64,1024]{1,0:T(8,128)(2,1)} %panel_one.1, bf16[64,1024]{1,0:T(8,128)(2,1)} %panel_two.1, bf16[512,512]{1,0:T(8,128)(2,1)} %inverse_one.1, bf16[512,512]{1,0:T(8,128)(2,1)} %inverse_two.1, ...), custom_call_target="tpu_custom_call" | custom-call | tf_op jit(solution)/shard_map/pallas_call | solution.py:462
  87.3 1.6 %copy.17 = bf16[64,1024]{1,0:T(8,128)(2,1)} copy(bf16[64,1024]{1,0:T(8,128)(2,1)} %get-tuple-element.12) | data formatting | bytes 262144
  88.9 1.6 %copy.18 = bf16[64,1024]{1,0:T(8,128)(2,1)} copy(bf16[64,1024]{1,0:T(8,128)(2,1)} %get-tuple-element.13) | data formatting | bytes 262144
  90.5 4.8 %copy.19 = bf16[1,1,128,128,128]{4,3,2,1,0:T(8,128)(2,1)} copy(bf16[1,1,128,128,128]{4,3,2,1,0:T(8,128)(2,1)} %bitcast.7) | data formatting | bytes 8388608

commit v2 on v1

--- a/solution.py
+++ b/solution.py
@@ -62,40 +62,144 @@
     return [(way, first if way == "z+" else second)] if abs(sz) == 3 else []
 
 
-def gather_plan(rate=47.0, latency=1.7):
+LINK_RATE, LATENCY, BACKLOG = 47.0, 2.0, 1.2
+
+
+def hops_left(way, piece, source):
+    sy, sz = next_source(source, way)
+    if piece[0] < PART_A[1]:
+        return 2 - abs(sy) if way[0] == "y" else 4 - abs(sz) + 2
+    return 4 - abs(sz) if way[0] == "z" else 2 - abs(sy) + 4
+
+
+def receives():
+    found, heap = [], [(w, p, next_source((0, 0), w)) for w, p in OWN_SENDS]
+    seen = {}
+    while heap:
+        way, piece, source = heap.pop(0)
+        found.append((way, piece, source))
+        seen.setdefault(source, set()).add(piece)
+        for onward, part in forwards(way, piece, source, seen[source]):
+            heap.append((onward, part, next_source(source, onward)))
+    return found
+
+
+EVENTS = receives()
+EVENT = {event: i for i, event in enumerate(EVENTS)}
+N_EVENTS = len(EVENTS)
+VMEM_LIMIT = 26 * 1024 * 1024
+FINISH_LIMIT = 6 * 1024 * 1024
+CHAIN = (
+    ("sum_y", None, 0.8, 0.15),
+    ("sum_back", "sum_y", 5.3, 0.15),
+    ("bridge_spread", "sum_back", 5.5, 0.05),
+    ("one_1", None, 7.0, 0.02),
+    ("one_3", None, 9.0, 0.02),
+    ("one_2", None, 9.5, 0.02),
+    ("one_side", "one_2", 2.2, 0.02),
+    ("two_1", None, 12.0, 0.02),
+    ("two_3", None, 13.0, 0.02),
+    ("two_2", None, 15.5, 0.02),
+    ("two_side", "two_2", 1.7, 0.02),
+    ("bridge_1", "bridge_spread", 5.0, 0.02),
+    ("bridge_3", "bridge_spread", 5.0, 0.02),
+    ("bridge_2", "bridge_spread", 6.5, 0.02),
+    ("bridge_side", "bridge_2", 1.7, 0.02),
+)
+
+
+def make_program():
     free = dict.fromkeys(STEP, 0.0)
-    seen, heap, plan = {}, [], []
-
-    def send(now, way, piece, source):
-        free[way] = max(now, free[way]) + piece[1] * 256 / 1000 / rate
-        heapq.heappush(
-            heap, (free[way] + latency, len(heap) + len(plan), way, piece, next_source(source, way))
-        )
-
-    for way, piece in OWN_SENDS:
-        send(0.0, way, piece, (0, 0))
-    while heap:
-        now, _, way, piece, source = heapq.heappop(heap)
-        seen.setdefault(source, set()).add(piece)
-        out = forwards(way, piece, source, seen[source])
-        plan.append((now, way, piece, source, out))
-        for onward, part in out:
-            send(now, onward, part, source)
-    return plan
-
-
-PLAN = gather_plan()
-EVENT = {(way, piece, source): i for i, (_, way, piece, source, _) in enumerate(PLAN)}
-N_EVENTS = len(PLAN)
-
-
-def tile_order():
-    rows, done = {}, []
-    for now, _, piece, source, _ in PLAN:
-        rows[source] = rows.get(source, 0) + piece[1]
-        if rows[source] == 512:
-            done.append((now, source))
-    return [(0.0, (0, 0))] + done
+    arriving, pending, seen, rows = [], {way: [] for way in STEP}, ({}, {}), ({}, {})
+    ready = ([(0, 0)], [])
+    program, ended, state = [], {}, {"now": 0.0, "count": 0, "products": [0, 0], "combined": 0}
+    chain = list(CHAIN)
+
+    def queue(p, way, piece, source):
+        state["count"] += 1
+        rank = (p, -hops_left(way, piece, source), state["count"])
+        heapq.heappush(pending[way], (rank, p, piece, source))
+
+    def ship(way):
+        _, p, piece, source = heapq.heappop(pending[way])
+        free[way] = max(free[way], state["now"]) + piece[1] * 256 / 1000 / LINK_RATE
+        heapq.heappush(arriving, (free[way] + LATENCY, state["count"], p, way, piece, next_source(source, way)))
+        state["count"] += 1
+        program.append(("send", p, way, piece, source))
+        state["now"] += 0.02
+
+    def receive():
+        _, _, p, way, piece, source = heapq.heappop(arriving)
+        program.append(("wait", p, way, piece, source))
+        state["now"] += 0.02
+        seen[p].setdefault(source, set()).add(piece)
+        rows[p][source] = rows[p].get(source, 0) + piece[1]
+        for onward, part in forwards(way, piece, source, seen[p][source]):
+            queue(p, onward, part, source)
+        if rows[p][source] == 512:
+            ready[p].append(source)
+
+    steps = [("factor_one", i, 0.53, "one_side") for i in range(4)]
+    steps += [("bridge_build", i, 0.5, "bridge_side") for i in range(4)]
+    steps += [("factor_two", i, 0.86, "two_side") for i in range(4)]
+    jobs = {name: [s for s in steps if s[0] == name] for name in ("factor_one", "bridge_build", "factor_two")}
+
+    def job():
+        for name, before in (("bridge_build", ()), ("factor_two", ("factor_one", "bridge_build")), ("factor_one", ())):
+            if jobs[name] and not any(jobs[b] for b in before) and jobs[name][0][3] in ended:
+                if ended[jobs[name][0][3]] <= state["now"] and (name != "factor_two" or "two_side" in ended):
+                    _, i, cost, _ = jobs[name].pop(0)
+                    return (name, i), cost
+        if not jobs["factor_one"] and len(ready[0]) >= 2:
+            return ("products", 0, ready[0].pop(0), ready[0].pop(0)), 0.65
+        if state["products"][0] == 16 and state["combined"] < 8:
+            state["combined"] += 1
+            return ("combine", state["combined"] - 1), 0.32
+        if state["combined"] == 8 and not jobs["factor_two"] and len(ready[1]) >= 2:
+            return ("products", 1, ready[1].pop(0), ready[1].pop(0)), 0.65
+        return None, 0.0
+
+    def begin(p):
+        for way, piece in OWN_SENDS:
+            queue(p, way, piece, (0, 0))
+
+    begin(0)
+    while True:
+        now = state["now"]
+        if arriving and arriving[0][0] <= now:
+            receive()
+            continue
+        ways = [w for w in STEP if pending[w] and free[w] - now < BACKLOG]
+        if ways:
+            ship(min(ways, key=lambda w: free[w]))
+            continue
+        due = [c for c in chain if (c[1] is None or c[1] in ended) and (ended.get(c[1], 0.0) + c[2] <= now)]
+        if due:
+            chain.remove(due[0])
+            program.append(("chain", due[0][0]))
+            state["now"] += due[0][3]
+            ended[due[0][0]] = state["now"]
+            continue
+        work, cost = job()
+        if work:
+            program.append(("job",) + work)
+            state["now"] += cost
+            if work[0] == "products":
+                state["products"][work[1]] += 1
+            if work == ("factor_two", 0):
+                ready[1].append((0, 0))
+                begin(1)
+            continue
+        later = [arriving[0][0]] if arriving else []
+        later += [free[w] - BACKLOG for w in STEP if pending[w]]
+        later += [ended.get(c[1], 0.0) + c[2] for c in chain if c[1] is None or c[1] in ended]
+        if not later:
+            break
+        state["now"] = max(now + 0.01, min(later))
+    return program, state["now"]
+
+
+PROGRAM, PLANNED = make_program()
 
 
 def kernel(
@@ -108,11 +212,11 @@
     row_map,
     rows_one,
     cols_one,
-    rows_two,
-    cols_two,
     lower_one,
     lower_two,
-    trailing,
+    upper,
+    lower,
+    partial,
     slab_one,
     slab_two,
     full_one,
@@ -131,11 +235,13 @@
     left_one,
     left_two,
     tiles,
-    products,
-    partial,
     staged,
+    bridge_from,
+    map_from,
+    pick_rows,
+    pick_cols,
     local_sem,
-    out_sem,
+    index_sem,
     x_send,
     x_recv,
     side_recv,
@@ -182,6 +288,10 @@
     load_inv_one = pltpu.make_async_copy(inverse_one, inv_one, local_sem.at[2])
     load_inv_two = pltpu.make_async_copy(inverse_two, inv_two, local_sem.at[3])
     load_targets = pltpu.make_async_copy(targets, staged, local_sem.at[4])
+    small = [(column_blocks, bridge_from), (row_map, map_from), (rows_one, pick_rows), (cols_one, pick_cols)]
+    small = [pltpu.make_async_copy(src, dst, index_sem.at[i]) for i, (src, dst) in enumerate(small)]
+    for copy in small:
+        copy.start()
     load_inv_one.start()
     load_inv_two.start()
     load_targets.start()
@@ -192,6 +302,8 @@
     along_y = [(row_at(d, 0), col) for d in range(1, NY)]
     for device in in_row + along_z + along_y:
         pl.semaphore_signal(barrier, inc=1, device_id=device, device_id_type=MESH)
+    for copy in small:
+        copy.wait()
     pltpu.make_async_copy(slab_one, slab_one, local_sem.at[0]).wait()
     pltpu.make_async_copy(slab_two, slab_two, local_sem.at[1]).wait()
     keep_one = pltpu.make_async_copy(slab_one, full_one.at[:, pl.ds(base, slab), :], local_sem.at[5])
@@ -208,7 +320,7 @@
         ).start()
 
     for k in range(4):
-        chosen = column_blocks[k]
+        chosen = bridge_from[k]
         block = slab_one[chosen % n_blocks]
         block = jnp.where(chosen // n_blocks == row, block.astype(f32), 0.0).astype(bf16)
         pick[2 * k] = block[:32]
@@ -268,15 +380,9 @@
         event = EVENT[(way, piece, next_source(source, way))]
         remote(ref, ref, tile_send.at[p], tile_recv.at[p, event], (row_at(*STEP[way]), col)).start()
 
-    def own_sends(p):
-        for way, piece in OWN_SENDS:
-            tile_copy(p, way, piece, (0, 0))
-
-    def tile_event(p, index):
-        _, _, piece, source, out = PLAN[index]
-        await_recv(tiles.at[p, row_at(*source), pl.ds(*piece), :], tile_recv.at[p, index])
-        for way, part in out:
-            tile_copy(p, way, part, source)
+    def tile_wait(p, way, piece, source):
+        ref = tiles.at[p, row_at(*source), pl.ds(*piece), :]
+        await_recv(ref, tile_recv.at[p, EVENT[(way, piece, source)]])
 
     def dot(a, b):
         return jnp.dot(a, b, preferred_element_type=f32)
@@ -291,36 +397,33 @@
             blocks[2 * i + h] = part.astype(bf16)
             left[pl.ds(pl.multiple_of((2 * i + h) * 128, 128), 128), :] = part.T.astype(bf16)
 
-    def factor_one():
-        @pl.loop(0, n_blocks // 2)
-        def _(i):
-            pair = jnp.concatenate([full_one[2 * i], full_one[2 * i + 1]], axis=1)
-            store_pair(blocks_one, left_one, i, dot(inv_one[...], pair))
-
-    def bridge_build():
-        @pl.loop(0, 4)
-        def _(k):
-            value = dot(inv_one[...], raw_bridge[k])
-            bridge_t[pl.ds(pl.multiple_of(k * 128, 128), 128), :] = value.T.astype(bf16)
+    def factor_one(i):
+        pair = jnp.concatenate([full_one[2 * i], full_one[2 * i + 1]], axis=1)
+        store_pair(blocks_one, left_one, i, dot(inv_one[...], pair))
+        if i == n_blocks // 2 - 1:
+            write_lower(blocks_one, lower_one)
+
+    def bridge_build(k):
+        value = dot(inv_one[...], raw_bridge[k])
+        bridge_t[k * 128 : (k + 1) * 128, :] = value.T.astype(bf16)
 
     def pair_two(i):
         mapped = jnp.concatenate(
-            [blocks_one[row_map[2 * i] % n_blocks], blocks_one[row_map[2 * i + 1] % n_blocks]], axis=1
+            [blocks_one[map_from[2 * i] % n_blocks], blocks_one[map_from[2 * i + 1] % n_blocks]], axis=1
         )
         pair = jnp.concatenate([full_two[2 * i], full_two[2 * i + 1]], axis=1)
         updated = (pair.astype(f32) - dot(bridge_t[...], mapped)).astype(bf16)
         store_pair(blocks_two, left_two, i, dot(inv_two[...], updated))
 
-    def factor_two_own():
-        pair_two(col // 2)
-        tiles[1, row] = blocks_two[col]
-
-    def factor_two_rest():
-        @pl.loop(1, n_blocks // 2)
-        def _(i):
-            pair_two((col // 2 + i) % (n_blocks // 2))
-
-    def products_of(p, left, first, second):
+    def factor_two(i):
+        pair_two((col // 2 + i) % (n_blocks // 2))
+        if i == 0:
+            tiles[1, row] = blocks_two[col]
+        if i == n_blocks // 2 - 1:
+            write_lower(blocks_two, lower_two)
+
+    def products_of(p, first, second):
+        left = (left_one, left_two)[p]
         t0, t1 = row_at(*first), row_at(*second)
 
         @pl.loop(0, 2)
@@ -328,102 +431,67 @@
             pair = jnp.concatenate([tiles[p, t0], tiles[p, t1]], axis=1)
             value = dot(left[pl.ds(pl.multiple_of(m * 512, 512), 512), :], pair)
             for h, t in enumerate((t0, t1)):
-                products[pl.ds(t * n_blocks + 4 * m, 4)] = value[:, h * 128 : (h + 1) * 128].reshape(4, 128, 128)
+                part = value[:, h * 128 : (h + 1) * 128].reshape(4, 128, 128)
+                upper[pl.ds(t * n_blocks + 4 * m, 4)] = part[:, :64]
+                lower[pl.ds(t * n_blocks + 4 * m, 4)] = part[:, 64:]
 
     n_slots = staged.shape[0]
 
-    def combine_one():
-        load_targets.wait()
-
-        @pl.loop(0, n_slots)
+    def combine(g):
+        if g == 0:
+            load_targets.wait()
+
+        @pl.loop(g * n_slots // 8, (g + 1) * n_slots // 8, unroll=4)
         def _(s):
-            index = (cols_one[s] // n_blocks) * n_blocks + rows_one[s] % n_blocks
-            partial[s] = staged[s].astype(f32) - products[index]
-
-    group = 16
-
-    def result_copy(g):
-        return pltpu.make_async_copy(
-            staged.at[pl.ds(g * group, group)], trailing.at[pl.ds(g * group, group)], out_sem.at[g]
-        )
-
-    def combine_two():
-        for g in range(n_slots // group):
-
-            @pl.loop(g * group, (g + 1) * group)
-            def _(s):
-                index = (cols_two[s] // n_blocks) * n_blocks + rows_two[s] % n_blocks
-                staged[s] = (partial[s] - products[index]).astype(bf16)
-
-            result_copy(g).start()
-
-    def write_lower(blocks, out, which):
-        return [
-            pltpu.make_async_copy(
-                blocks.at[j, pl.ds(base, slab), :], out.at[:, pl.ds(j * 128, 128)], local_sem.at[8 + which]
-            )
-            for j in range(n_blocks)
-        ]
-
-    def start_all(copies):
-        for copy in copies:
-            copy.start()
-
-    lower_copies = write_lower(blocks_one, lower_one, 0) + write_lower(blocks_two, lower_two, 1)
+            index = (pick_cols[s] // n_blocks) * n_blocks + pick_rows[s] % n_blocks
+            partial[s, :64] = staged[s, :64].astype(f32) - upper[index]
+            partial[s, 64:] = staged[s, 64:].astype(f32) - lower[index]
+
+    def write_lower(blocks, out):
+        for j in range(n_blocks):
+            out[:, j * 128 : (j + 1) * 128] = blocks[j, pl.ds(base, slab), :]
+
+    chain = {
+        "sum_y": sum_y_send,
+        "sum_back": sum_z_return,
+        "bridge_spread": bridge_spread,
+        "one_side": lambda: side_wait(full_one, 0),
+        "two_side": lambda: side_wait(full_two, 1),
+        "bridge_side": lambda: side_wait(raw_bridge, 2),
+    }
+    for which, (name, full) in enumerate((("one", full_one), ("two", full_two), ("bridge", raw_bridge))):
+        for dx in range(1, NX):
+            chain[f"{name}_{dx}"] = functools.partial(pass_on, full, which, dx)
+    jobs = {
+        "factor_one": factor_one,
+        "bridge_build": bridge_build,
+        "factor_two": factor_two,
+        "products": products_of,
+        "combine": combine,
+    }
 
     sum_z_send()
-    spread(slab_one, full_one, 0)
-    spread(slab_two, full_two, 1)
     load_inv_one.wait()
     load_inv_two.wait()
     keep_raw.wait()
     keep_one.wait()
     keep_two.wait()
     first_block()
-    own_sends(0)
-
-    one, two = 0.0, 18.5
-    work = [
-        (0.6, sum_y_send),
-        (3.6, sum_z_return),
-        (4.0, lambda: pass_on(full_one, 0, 1)),
-        (4.1, lambda: pass_on(full_one, 0, 3)),
-        (4.9, lambda: pass_on(full_one, 0, 2)),
-        (6.5, lambda: side_wait(full_one, 0)),
-        (6.6, factor_one),
-        (6.7, lambda: start_all(lower_copies[:n_blocks])),
-        (8.6, bridge_spread),
-        (9.0, lambda: pass_on(full_two, 1, 1)),
-        (9.1, lambda: pass_on(full_two, 1, 3)),
-        (10.6, lambda: pass_on(full_two, 1, 2)),
-        (12.2, lambda: side_wait(full_two, 1)),
-        (13.8, lambda: pass_on(raw_bridge, 2, 1)),
-        (13.9, lambda: pass_on(raw_bridge, 2, 3)),
-        (14.8, lambda: pass_on(raw_bridge, 2, 2)),
-        (16.3, lambda: side_wait(raw_bridge, 2)),
-        (16.4, bridge_build),
-        (16.5, factor_two_own),
-        (16.6, lambda: own_sends(1)),
-        (16.7, factor_two_rest),
-        (16.8, lambda: start_all(lower_copies[n_blocks:])),
-    ]
-    for i, (now, *_) in enumerate(PLAN):
-        work.append((one + now, functools.partial(tile_event, 0, i)))
-        work.append((two + now, functools.partial(tile_event, 1, i)))
-    order = tile_order()
-    for i in range(0, len(order), 2):
-        now, pair = order[i + 1][0], (order[i][1], order[i + 1][1])
-        work.append((max(one + now, 6.61) + 0.01, functools.partial(products_of, 0, left_one, *pair)))
-        work.append((max(two + now, one + PLAN[-1][0] + 0.1) + 0.01, functools.partial(products_of, 1, left_two, *pair)))
-    work.append((one + PLAN[-1][0] + 0.1, combine_one))
-    for _, step in sorted(work, key=lambda item: item[0]):
-        step()
-    combine_two()
-
-    for g in range(n_slots // group):
-        result_copy(g).wait()
-    pltpu.make_async_copy(lower_one, lower_one, local_sem.at[8]).wait()
-    pltpu.make_async_copy(lower_two, lower_two, local_sem.at[9]).wait()
+    started = False
+    for kind, *what in PROGRAM:
+        if kind == "send":
+            tile_copy(*what)
+        elif kind == "wait":
+            if not started:
+                spread(slab_one, full_one, 0)
+                spread(slab_two, full_two, 1)
+                started = True
+            tile_wait(*what)
+        elif kind == "chain":
+            chain[what[0]]()
+        else:
+            jobs[what[0]](*what[1:])
+
     await_send(own_raw.at[pl.ds(0, (NX * NC - 1) * slab), :], swap_send)
     await_send(ring_z, sum_send.at[0])
     await_send(ring_y, sum_send.at[1])
@@ -433,6 +501,40 @@
     await_send(full_two.at[pl.ds(0, n_blocks - 1), pl.ds(0, 256), :], x_send.at[2])
     await_send(tiles.at[0, pl.ds(0, NY * NZ - 1)], tile_send.at[0])
     await_send(tiles.at[1, pl.ds(0, NY * NZ - 1)], tile_send.at[1])
+
+
+GROUP = 16
+
+
+def finish_kernel(
+    rows_in, cols_in, lower_one, lower_two, upper, lower, partial, out_one, out_two, trailing, staged, rows, cols, sem
+):
+    index = [pltpu.make_async_copy(rows_in, rows, sem.at[2]), pltpu.make_async_copy(cols_in, cols, sem.at[3])]
+    for copy in index:
+        copy.start()
+    n_slots = partial.shape[0]
+    n_blocks = lower_one.shape[1] // partial.shape[-1]
+    copies = [
+        pltpu.make_async_copy(lower_one, out_one, sem.at[0]),
+        pltpu.make_async_copy(lower_two, out_two, sem.at[1]),
+    ]
+    for copy in copies:
+        copy.start()
+    for copy in index:
+        copy.wait()
+    for g in range(n_slots // GROUP):
+
+        @pl.loop(g * GROUP, (g + 1) * GROUP, unroll=4)
+        def _(s):
+            index = (cols[s] // n_blocks) * n_blocks + rows[s] % n_blocks
+            staged[s, :64] = (partial[s, :64] - upper[index]).astype(staged.dtype)
+            staged[s, 64:] = (partial[s, 64:] - lower[index]).astype(staged.dtype)
+
+        part = pl.ds(g * GROUP, GROUP)
+        copies.append(pltpu.make_async_copy(staged.at[part], trailing.at[part], sem.at[4 + g]))
+        copies[-1].start()
+    for copy in copies:
+        copy.wait()
 
 
 def per_device(
@@ -457,17 +559,24 @@
     bf16, f32 = jnp.bfloat16, jnp.float32
     vmem = pltpu.VMEM
     dma = pltpu.SemaphoreType.DMA
-    in_hbm = pl.BlockSpec(memory_space=pl.ANY)
-    in_smem = pl.BlockSpec(memory_space=pltpu.SMEM)
-    lower_one, lower_two, trailing = pl.pallas_call(
+    in_hbm = pl.BlockSpec(memory_space=pltpu.HBM)
+    smem = pltpu.SMEM
+    in_vmem = pl.BlockSpec(memory_space=vmem)
+
+    def stay(*arrays):
+        return [pltpu.with_memory_space_constraint(array, pltpu.HBM) for array in arrays]
+
+    held = pl.pallas_call(
         kernel,
         out_shape=(
-            jax.ShapeDtypeStruct(panel_one.shape, bf16),
-            jax.ShapeDtypeStruct(panel_two.shape, bf16),
-            jax.ShapeDtypeStruct((n_slots, size, size), bf16),
+            vmem(panel_one.shape, bf16),
+            vmem(panel_two.shape, bf16),
+            vmem((n_rows * n_blocks, size // 2, size), f32),
+            vmem((n_rows * n_blocks, size // 2, size), f32),
+            vmem((n_slots, size, size), f32),
         ),
-        in_specs=[in_hbm] * 5 + [in_smem] * 6,
-        out_specs=(in_hbm,) * 3,
+        in_specs=[in_hbm] * 9,
+        out_specs=(in_vmem,) * 5,
         scratch_shapes=[
             vmem((n_blocks, slab, size), bf16),
             vmem((n_blocks, slab, size), bf16),
@@ -487,11 +596,13 @@
             vmem((row_count, width), bf16),
             vmem((row_count, width), bf16),
             vmem((2, n_rows, width, size), bf16),
-            vmem((n_rows * n_blocks, size, size), f32),
-            vmem((n_slots, size, size), f32),
             vmem((n_slots, size, size), bf16),
-            dma((10,)),
+            smem((4,), jnp.int32),
+            smem((n_blocks,), jnp.int32),
+            smem((n_slots,), jnp.int32),
+            smem((n_slots,), jnp.int32),
             dma((8,)),
+            dma((4,)),
             dma((3,)),
             dma((3, NX - 1)),
             dma((3,)),
@@ -503,21 +614,38 @@
             dma((2, N_EVENTS)),
         ],
         compiler_params=pltpu.CompilerParams(
-            collective_id=0, has_side_effects=True, vmem_limit_bytes=62 * 1024 * 1024
+            collective_id=0, has_side_effects=True, vmem_limit_bytes=VMEM_LIMIT
         ),
     )(
-        panel_one,
-        panel_two,
-        inverse_one,
-        inverse_two,
-        targets.reshape(n_slots, size, size),
-        column_blocks,
-        row_map,
-        rows_one.reshape(-1),
-        cols_one.reshape(-1),
-        rows_two.reshape(-1),
-        cols_two.reshape(-1),
+        *stay(
+            panel_one,
+            panel_two,
+            inverse_one,
+            inverse_two,
+            targets.reshape(n_slots, size, size),
+            column_blocks,
+            row_map,
+            rows_one.reshape(-1),
+            cols_one.reshape(-1),
+        )
     )
+    lower_one, lower_two, trailing = pl.pallas_call(
+        finish_kernel,
+        out_shape=(
+            jax.ShapeDtypeStruct(panel_one.shape, bf16),
+            jax.ShapeDtypeStruct(panel_two.shape, bf16),
+            jax.ShapeDtypeStruct((n_slots, size, size), bf16),
+        ),
+        in_specs=[in_hbm] * 2 + [in_vmem] * 5,
+        out_specs=(in_hbm,) * 3,
+        scratch_shapes=[
+            vmem((n_slots, size, size), bf16),
+            smem((n_slots,), jnp.int32),
+            smem((n_slots,), jnp.int32),
+            dma((4 + n_slots // GROUP,)),
+        ],
+        compiler_params=pltpu.CompilerParams(vmem_limit_bytes=FINISH_LIMIT),
+    )(*stay(rows_two.reshape(-1), cols_two.reshape(-1)), *held)
     return lower_one, lower_two, trailing.reshape(targets.shape)
 
 

time: 97 us -> 77.7 us (0.80); the launches traced: 95.2 us -> 77.6 us
  Pallas kernels: 86.7 us -> 76.9 us
  local copies, waits for them, and re-layouts: 7.92 us -> 0 us
    pallas_call x1 -> x2, Pallas kernels: 86.7 us -> 76.9 us  [the longest x1 73.9 us: per_device(): pl.pallas_call(kernel, out_shape=(vmem(panel_one.shape, bf16), vmem(panel...]
    unnamed x3 -> x0, local copies, waits for them, and re-layouts: 7.92 us -> none
where the time goes in v2:
time: 77.7 us; the launch traced here: 77.6 us
  Pallas kernels  76.9 us (99%)
    pallas_call x1, Pallas kernels, per_device(): pl.pallas_call(kernel, out_shape=(vmem(panel_one.shape, bf16), vmem(panel...  73.9 us
    pallas_call x1, Pallas kernels, per_device(): pl.pallas_call(finish_kernel, out_shape=(jax.ShapeDtypeStruct(panel_one.s...  2.99 us

profile of v2, /device:TPU:2, one launch (start us, length us, event | category | flops | bytes accessed | tf_op | source)
XLA Modules:
  0.0 77.6 jit_solution(3718827223250304639)
XLA Ops:
  0.6 73.9 %shard_map.130 = (bf16[64,1024]{1,0:T(8,128)(2,1)S(1)}, bf16[64,1024]{1,0:T(8,128)(2,1)S(1)}, f32[256,64,128]{2,1,0:T(8,128)S(1)}, f32[256,64,128]{2,1,0:T(8,128)S(1)}, f32[128,128,128]{2,1,0:T(8,128)S(1)}) custom-call(bf16[64,1024]{1,0:T(8,128)(2,1)} %panel_one.1, bf16[64,1024]{1,0:T(8,128)(2,1)} %panel_two.1, bf16[512,512]{1,0:T(8,128)(2,1)} %inverse_one.1, ...), custom_call_target="tpu_custom_call" | custom-call | tf_op jit(solution)/shard_map/pallas_call | solution.py:569
  74.6 3.0 %shard_map.131 = (bf16[64,1024]{1,0:T(8,128)(2,1)}, bf16[64,1024]{1,0:T(8,128)(2,1)}, bf16[128,128,128]{2,1,0:T(8,128)(2,1)}) custom-call(s32[128]{0:T(128)} %bitcast.7, s32[128]{0:T(128)} %bitcast.8, bf16[64,1024]{1,0:T(8,128)(2,1)S(1)} %get-tuple-element.11.lower_one, bf16[64,1024]{1,0:T(8,128)(2,1)S(1)} %get-tuple-element.12.lower_two, ...), custom_call_target="tpu_custom_call" | custom-call | tf_op jit(solution)/shard_map/pallas_call | solution.py:632

commit v3 on v2

--- a/solution.py
+++ b/solution.py
@@ -62,7 +62,7 @@
     return [(way, first if way == "z+" else second)] if abs(sz) == 3 else []
 
 
-LINK_RATE, LATENCY, BACKLOG = 47.0, 2.0, 1.2
+LINK_RATE, LATENCY, BACKLOG, PANEL_WEIGHT = 47.0, 2.6, 0.6, 100.0
 
 
 def hops_left(way, piece, source):
@@ -87,24 +87,23 @@
 EVENTS = receives()
 EVENT = {event: i for i, event in enumerate(EVENTS)}
 N_EVENTS = len(EVENTS)
-VMEM_LIMIT = 26 * 1024 * 1024
+VMEM_LIMIT = 34 * 1024 * 1024
 FINISH_LIMIT = 6 * 1024 * 1024
 CHAIN = (
-    ("sum_y", None, 0.8, 0.15),
-    ("sum_back", "sum_y", 5.3, 0.15),
-    ("bridge_spread", "sum_back", 5.5, 0.05),
-    ("one_1", None, 7.0, 0.02),
-    ("one_3", None, 9.0, 0.02),
-    ("one_2", None, 9.5, 0.02),
-    ("one_side", "one_2", 2.2, 0.02),
-    ("two_1", None, 12.0, 0.02),
-    ("two_3", None, 13.0, 0.02),
-    ("two_2", None, 15.5, 0.02),
-    ("two_side", "two_2", 1.7, 0.02),
-    ("bridge_1", "bridge_spread", 5.0, 0.02),
-    ("bridge_3", "bridge_spread", 5.0, 0.02),
-    ("bridge_2", "bridge_spread", 6.5, 0.02),
-    ("bridge_side", "bridge_2", 1.7, 0.02),
+    ("sum_back", None, 3.9, 0.15),
+    ("bridge_spread", "sum_back", 5.8, 0.05),
+    ("one_1", None, 6.0, 0.02),
+    ("one_3", None, 6.0, 0.02),
+    ("one_2", None, 10.2, 0.02),
+    ("one_side", "one_2", 2.8, 0.02),
+    ("two_1", None, 9.0, 0.02),
+    ("two_3", None, 9.0, 0.02),
+    ("two_2", None, 12.5, 0.02),
+    ("two_side", "two_2", 2.8, 0.02),
+    ("bridge_1", "bridge_spread", 4.3, 0.02),
+    ("bridge_3", "bridge_spread", 4.3, 0.02),
+    ("bridge_2", "bridge_3", 3.3, 0.02),
+    ("bridge_side", "bridge_2", 2.0, 0.02),
 )
 
 
@@ -117,7 +116,7 @@
 
     def queue(p, way, piece, source):
         state["count"] += 1
-        rank = (p, -hops_left(way, piece, source), state["count"])
+        rank = (PANEL_WEIGHT * p - hops_left(way, piece, source), state["count"])
         heapq.heappush(pending[way], (rank, p, piece, source))
 
     def ship(way):
@@ -140,7 +139,7 @@
             ready[p].append(source)
 
     steps = [("factor_one", i, 0.53, "one_side") for i in range(4)]
-    steps += [("bridge_build", i, 0.5, "bridge_side") for i in range(4)]
+    steps += [("bridge_build", i, 0.55, "bridge_side") for i in range(2)]
     steps += [("factor_two", i, 0.86, "two_side") for i in range(4)]
     jobs = {name: [s for s in steps if s[0] == name] for name in ("factor_one", "bridge_build", "factor_two")}
 
@@ -150,13 +149,13 @@
                 if ended[jobs[name][0][3]] <= state["now"] and (name != "factor_two" or "two_side" in ended):
                     _, i, cost, _ = jobs[name].pop(0)
                     return (name, i), cost
-        if not jobs["factor_one"] and len(ready[0]) >= 2:
-            return ("products", 0, ready[0].pop(0), ready[0].pop(0)), 0.65
-        if state["products"][0] == 16 and state["combined"] < 8:
-            state["combined"] += 1
-            return ("combine", state["combined"] - 1), 0.32
-        if state["combined"] == 8 and not jobs["factor_two"] and len(ready[1]) >= 2:
-            return ("products", 1, ready[1].pop(0), ready[1].pop(0)), 0.65
+        free_to_run = (not jobs["factor_one"], state["combined"] == 8 and not jobs["factor_two"])
+        for p in range(2):
+            if free_to_run[p] and len(ready[p]) >= 2:
+                return ("products", p) + (ready[p].pop(0), ready[p].pop(0)), 0.52
+            if p == 0 and state["products"][0] == 32 and state["combined"] < 8:
+                state["combined"] += 1
+                return ("combine", state["combined"] - 1), 0.2
         return None, 0.0
 
     def begin(p):
@@ -185,7 +184,7 @@
             program.append(("job",) + work)
             state["now"] += cost
             if work[0] == "products":
-                state["products"][work[1]] += 1
+                state["products"][work[1]] += len(work) - 2
             if work == ("factor_two", 0):
                 ready[1].append((0, 0))
                 begin(1)
@@ -232,8 +231,7 @@
     bridge_t,
     blocks_one,
     blocks_two,
-    left_one,
-    left_two,
+    left,
     tiles,
     staged,
     bridge_from,
@@ -326,18 +324,27 @@
         pick[2 * k] = block[:32]
         pick[2 * k + 1] = block[32:]
 
+    def slab_of(full, dx):
+        return full.at[:, pl.ds(pl.multiple_of(col_at(NX - dx) * slab, slab), slab), :]
+
     def spread(mine, full, which):
-        for dx in range(1, NX):
+        place = full.at[:, pl.ds(base, slab), :]
+        for dx in (1, 3):
+            remote(mine, place, x_send.at[which], x_recv.at[which, dx - 1], (row, col_at(dx))).start()
+        remote(mine, place, x_send.at[which], side_recv.at[which], (row, partner)).start()
+
+    def pass_on(full, which, dx):
+        ref = slab_of(full, dx)
+        half = full.shape[0] // 2
+        if dx == 2:
+            await_recv(ref.at[pl.ds(0, half)], x_recv.at[which, 1])
+            await_recv(ref.at[pl.ds(half, half)], x_recv.at[which, 3])
+        else:
+            await_recv(ref, x_recv.at[which, dx - 1])
+            part = ref.at[pl.ds(0 if dx == 1 else half, half)]
             remote(
-                mine, full.at[:, pl.ds(base, slab), :], x_send.at[which], x_recv.at[which, dx - 1], (row, col_at(dx))
+                part, part, x_send.at[which], x_recv.at[which, 1 if dx == 1 else 3], (row, col_at(dx))
             ).start()
-        remote(
-            mine, full.at[:, pl.ds(base, slab), :], x_send.at[which], side_recv.at[which], (row, partner)
-        ).start()
-
-    def pass_on(full, which, dx):
-        ref = full.at[:, pl.ds(pl.multiple_of(col_at(NX - dx) * slab, slab), slab), :]
-        await_recv(ref, x_recv.at[which, dx - 1])
         remote(ref, ref, x_send.at[which], side_recv.at[which], (row, partner)).start()
 
     def side_wait(full, which):
@@ -391,21 +398,21 @@
         await_recv(own_raw.at[pl.ds(0, (NX * NC - 1) * slab), :], swap_recv)
         tiles[0, row] = dot(inv_one[...], own_raw[...]).astype(bf16)
 
-    def store_pair(blocks, left, i, value):
+    def store_pair(blocks, p, i, value):
         for h in range(2):
             part = value[:, h * 128 : (h + 1) * 128]
             blocks[2 * i + h] = part.astype(bf16)
-            left[pl.ds(pl.multiple_of((2 * i + h) * 128, 128), 128), :] = part.T.astype(bf16)
+            left[p, pl.ds(pl.multiple_of((2 * i + h) * 128, 128), 128), :] = part.T.astype(bf16)
 
     def factor_one(i):
         pair = jnp.concatenate([full_one[2 * i], full_one[2 * i + 1]], axis=1)
-        store_pair(blocks_one, left_one, i, dot(inv_one[...], pair))
+        store_pair(blocks_one, 0, i, dot(inv_one[...], pair))
         if i == n_blocks // 2 - 1:
             write_lower(blocks_one, lower_one)
 
-    def bridge_build(k):
-        value = dot(inv_one[...], raw_bridge[k])
-        bridge_t[k * 128 : (k + 1) * 128, :] = value.T.astype(bf16)
+    def bridge_build(i):
+        pair = jnp.concatenate([raw_bridge[2 * i], raw_bridge[2 * i + 1]], axis=1)
+        bridge_t[i * 256 : (i + 1) * 256, :] = dot(inv_one[...], pair).T.astype(bf16)
 
     def pair_two(i):
         mapped = jnp.concatenate(
@@ -413,7 +420,7 @@
         )
         pair = jnp.concatenate([full_two[2 * i], full_two[2 * i + 1]], axis=1)
         updated = (pair.astype(f32) - dot(bridge_t[...], mapped)).astype(bf16)
-        store_pair(blocks_two, left_two, i, dot(inv_two[...], updated))
+        store_pair(blocks_two, 1, i, dot(inv_two[...], updated))
 
     def factor_two(i):
         pair_two((col // 2 + i) % (n_blocks // 2))
@@ -422,18 +429,12 @@
         if i == n_blocks // 2 - 1:
             write_lower(blocks_two, lower_two)
 
-    def products_of(p, first, second):
-        left = (left_one, left_two)[p]
-        t0, t1 = row_at(*first), row_at(*second)
-
-        @pl.loop(0, 2)
-        def _(m):
-            pair = jnp.concatenate([tiles[p, t0], tiles[p, t1]], axis=1)
-            value = dot(left[pl.ds(pl.multiple_of(m * 512, 512), 512), :], pair)
-            for h, t in enumerate((t0, t1)):
-                part = value[:, h * 128 : (h + 1) * 128].reshape(4, 128, 128)
-                upper[pl.ds(t * n_blocks + 4 * m, 4)] = part[:, :64]
-                lower[pl.ds(t * n_blocks + 4 * m, 4)] = part[:, 64:]
+    def products_of(p, rows):
+        value = dot(left[p], jnp.concatenate([tiles[p, t] for t in rows], axis=1))
+        for h, t in enumerate(rows):
+            part = value[:, h * 128 : (h + 1) * 128].reshape(n_blocks, 128, 128)
+            upper[pl.ds(t * n_blocks, n_blocks)] = part[:, :64]
+            lower[pl.ds(t * n_blocks, n_blocks)] = part[:, 64:]
 
     n_slots = staged.shape[0]
 
@@ -452,7 +453,6 @@
             out[:, j * 128 : (j + 1) * 128] = blocks[j, pl.ds(base, slab), :]
 
     chain = {
-        "sum_y": sum_y_send,
         "sum_back": sum_z_return,
         "bridge_spread": bridge_spread,
         "one_side": lambda: side_wait(full_one, 0),
@@ -466,7 +466,6 @@
         "factor_one": factor_one,
         "bridge_build": bridge_build,
         "factor_two": factor_two,
-        "products": products_of,
         "combine": combine,
     }
 
@@ -477,20 +476,46 @@
     keep_one.wait()
     keep_two.wait()
     first_block()
-    started = False
-    for kind, *what in PROGRAM:
-        if kind == "send":
-            tile_copy(*what)
-        elif kind == "wait":
-            if not started:
-                spread(slab_one, full_one, 0)
-                spread(slab_two, full_two, 1)
-                started = True
-            tile_wait(*what)
-        elif kind == "chain":
-            chain[what[0]]()
+    sum_y_send()
+    cuts, chosen = [[]], []
+    for op in PROGRAM:
+        if op[:2] == ("job", "products"):
+            chosen.append(op[3:])
+            cuts.append([])
         else:
-            jobs[what[0]](*what[1:])
+            cuts[-1].append(op)
+    cuts.pop()
+
+    def run(ops):
+        for kind, *what in ops:
+            if kind == "send":
+                tile_copy(*what)
+            elif kind == "wait":
+                tile_wait(*what)
+            elif kind == "chain":
+                chain[what[0]]()
+            else:
+                jobs[what[0]](*what[1:])
+
+    def run_cut(i, first, last):
+        if last - first == 1:
+            run(cuts[first])
+            return tuple(row_at(*source) for source in chosen[first])
+        middle = (first + last) // 2
+        return lax.cond(
+            i < middle, lambda: run_cut(i, first, middle), lambda: run_cut(i, middle, last)
+        )
+
+    starts = next(i for i, op in enumerate(cuts[0]) if op[0] != "send")
+    run(cuts[0][:starts])
+    cuts[0] = cuts[0][starts:]
+    spread(slab_one, full_one, 0)
+    spread(slab_two, full_two, 1)
+
+    @pl.loop(0, len(cuts))
+    def _(i):
+        rows = run_cut(i, 0, len(cuts))
+        products_of(i // (len(cuts) // 2), rows)
 
     await_send(own_raw.at[pl.ds(0, (NX * NC - 1) * slab), :], swap_send)
     await_send(ring_z, sum_send.at[0])
@@ -593,8 +618,7 @@
             vmem((width, width), bf16),
             vmem((n_blocks, width, size), bf16),
             vmem((n_blocks, width, size), bf16),
-            vmem((row_count, width), bf16),
-            vmem((row_count, width), bf16),
+            vmem((2, row_count, width), bf16),
             vmem((2, n_rows, width, size), bf16),
             vmem((n_slots, size, size), bf16),
             smem((4,), jnp.int32),
@@ -604,7 +628,7 @@
             dma((8,)),
             dma((4,)),
             dma((3,)),
-            dma((3, NX - 1)),
+            dma((3, NX)),
             dma((3,)),
             dma,
             dma,

time: 77.7 us -> 71.3 us (0.918)
  Pallas kernels: 76.9 us -> 70.6 us
    pallas_call x1, Pallas kernels: 73.9 us -> 67.6 us  [per_device(): pl.pallas_call(kernel, out_shape=(vmem(panel_one.shape, bf16), vmem(panel...]
where the time goes in v3:
time: 71.3 us; the launch traced here: 71.2 us
  Pallas kernels  70.6 us (99%)
    pallas_call x1, Pallas kernels, per_device(): pl.pallas_call(kernel, out_shape=(vmem(panel_one.shape, bf16), vmem(panel...  67.6 us
    pallas_call x1, Pallas kernels, per_device(): pl.pallas_call(finish_kernel, out_shape=(jax.ShapeDtypeStruct(panel_one.s...  2.99 us

profile of v3, /device:TPU:2, one launch (start us, length us, event | category | flops | bytes accessed | tf_op | source)
XLA Modules:
  0.0 71.2 jit_solution(1394365404753178705)
XLA Ops:
  0.6 67.6 %shard_map.130 = (bf16[64,1024]{1,0:T(8,128)(2,1)S(1)}, bf16[64,1024]{1,0:T(8,128)(2,1)S(1)}, f32[256,64,128]{2,1,0:T(8,128)S(1)}, f32[256,64,128]{2,1,0:T(8,128)S(1)}, f32[128,128,128]{2,1,0:T(8,128)S(1)}) custom-call(bf16[64,1024]{1,0:T(8,128)(2,1)} %panel_one.1, bf16[64,1024]{1,0:T(8,128)(2,1)} %panel_two.1, bf16[512,512]{1,0:T(8,128)(2,1)} %inverse_one.1, ...), custom_call_target="tpu_custom_call" | custom-call | tf_op jit(solution)/shard_map/pallas_call | solution.py:594
  68.2 3.0 %shard_map.131 = (bf16[64,1024]{1,0:T(8,128)(2,1)}, bf16[64,1024]{1,0:T(8,128)(2,1)}, bf16[128,128,128]{2,1,0:T(8,128)(2,1)}) custom-call(s32[128]{0:T(128)} %bitcast.7, s32[128]{0:T(128)} %bitcast.8, bf16[64,1024]{1,0:T(8,128)(2,1)S(1)} %get-tuple-element.11.lower_one, bf16[64,1024]{1,0:T(8,128)(2,1)S(1)} %get-tuple-element.12.lower_two, ...), custom_call_target="tpu_custom_call" | custom-call | tf_op jit(solution)/shard_map/pallas_call | solution.py:656

commit v4 on v3

--- a/solution.py
+++ b/solution.py
@@ -62,7 +62,8 @@
     return [(way, first if way == "z+" else second)] if abs(sz) == 3 else []
 
 
-LINK_RATE, LATENCY, BACKLOG, PANEL_WEIGHT = 47.0, 2.6, 0.6, 100.0
+LINK_RATE, LATENCY, BACKLOG, PANEL_WEIGHT = 47.0, 2.8, 0.5, 0.5
+SPREAD, MIX = 1.5, 41
 
 
 def hops_left(way, piece, source):
@@ -90,20 +91,20 @@
 VMEM_LIMIT = 34 * 1024 * 1024
 FINISH_LIMIT = 6 * 1024 * 1024
 CHAIN = (
-    ("sum_back", None, 3.9, 0.15),
-    ("bridge_spread", "sum_back", 5.8, 0.05),
-    ("one_1", None, 6.0, 0.02),
-    ("one_3", None, 6.0, 0.02),
-    ("one_2", None, 10.2, 0.02),
-    ("one_side", "one_2", 2.8, 0.02),
-    ("two_1", None, 9.0, 0.02),
-    ("two_3", None, 9.0, 0.02),
-    ("two_2", None, 12.5, 0.02),
-    ("two_side", "two_2", 2.8, 0.02),
-    ("bridge_1", "bridge_spread", 4.3, 0.02),
-    ("bridge_3", "bridge_spread", 4.3, 0.02),
-    ("bridge_2", "bridge_3", 3.3, 0.02),
-    ("bridge_side", "bridge_2", 2.0, 0.02),
+    ("sum_back", None, 4.4, 0.15),
+    ("bridge_spread", "sum_back", 5.4, 0.05),
+    ("one_1", None, 6.5, 0.02),
+    ("one_3", None, 6.5, 0.02),
+    ("one_2", None, 10.7, 0.02),
+    ("one_side", "one_2", 2.4, 0.02),
+    ("two_1", None, 9.5, 0.02),
+    ("two_3", None, 9.5, 0.02),
+    ("two_2", None, 13.0, 0.02),
+    ("two_side", "two_2", 2.4, 0.02),
+    ("bridge_1", "bridge_spread", 3.9, 0.02),
+    ("bridge_3", "bridge_spread", 3.9, 0.02),
+    ("bridge_2", "bridge_3", 2.9, 0.02),
+    ("bridge_side", "bridge_2", 1.6, 0.02),
 )
 
 
@@ -116,7 +117,8 @@
 
     def queue(p, way, piece, source):
         state["count"] += 1
-        rank = (PANEL_WEIGHT * p - hops_left(way, piece, source), state["count"])
+        vary = SPREAD * (state["count"] * MIX % 97) / 97
+        rank = (PANEL_WEIGHT * p - hops_left(way, piece, source) + vary, state["count"])
         heapq.heappush(pending[way], (rank, p, piece, source))
 
     def ship(way):
@@ -152,7 +154,7 @@
         free_to_run = (not jobs["factor_one"], state["combined"] == 8 and not jobs["factor_two"])
         for p in range(2):
             if free_to_run[p] and len(ready[p]) >= 2:
-                return ("products", p) + (ready[p].pop(0), ready[p].pop(0)), 0.52
+                return ("products", p) + (ready[p].pop(0), ready[p].pop(0)), 0.48
             if p == 0 and state["products"][0] == 32 and state["combined"] < 8:
                 state["combined"] += 1
                 return ("combine", state["combined"] - 1), 0.2
@@ -276,6 +278,13 @@
     def await_send(ref, sem):
         remote(ref, ref, sem, tile_recv.at[0, 0], (row, partner)).wait_send()
 
+    barrier = pltpu.get_barrier_semaphore()
+    in_row = [(row, (col + d) % (NX * NC)) for d in range(1, NX * NC)]
+    along_z = [(row_at(0, d), col) for d in range(1, NZ)]
+    along_y = [(row_at(d, 0), col) for d in range(1, NY)]
+    for device in in_row + along_z + along_y:
+        pl.semaphore_signal(barrier, inc=1, device_id=device, device_id_type=MESH)
+
     loads = []
     n_blocks = slab_one.shape[0]
     for which, (panel, mine) in enumerate(((panel_one, slab_one), (panel_two, slab_two))):
@@ -294,12 +303,6 @@
     load_inv_two.start()
     load_targets.start()
 
-    barrier = pltpu.get_barrier_semaphore()
-    in_row = [(row, (col + d) % (NX * NC)) for d in range(1, NX * NC)]
-    along_z = [(row_at(0, d), col) for d in range(1, NZ)]
-    along_y = [(row_at(d, 0), col) for d in range(1, NY)]
-    for device in in_row + along_z + along_y:
-        pl.semaphore_signal(barrier, inc=1, device_id=device, device_id_type=MESH)
     for copy in small:
         copy.wait()
     pltpu.make_async_copy(slab_one, slab_one, local_sem.at[0]).wait()

time: 71.3 us -> 70.4 us (0.987)
  Pallas kernels: 70.6 us -> 69.6 us
    pallas_call x1, Pallas kernels: 67.6 us -> 66.6 us  [per_device(): pl.pallas_call(kernel, out_shape=(vmem(panel_one.shape, bf16), vmem(panel...]
where the time goes in v4:
time: 70.4 us; the launch traced here: 70.2 us
  Pallas kernels  69.6 us (99%)
    pallas_call x1, Pallas kernels, per_device(): pl.pallas_call(kernel, out_shape=(vmem(panel_one.shape, bf16), vmem(panel...  66.6 us
    pallas_call x1, Pallas kernels, per_device(): pl.pallas_call(finish_kernel, out_shape=(jax.ShapeDtypeStruct(panel_one.s...  2.99 us

profile of v4, /device:TPU:2, one launch (start us, length us, event | category | flops | bytes accessed | tf_op | source)
XLA Modules:
  0.0 70.2 jit_solution(9207472574589695263)
XLA Ops:
  0.6 66.6 %shard_map.130 = (bf16[64,1024]{1,0:T(8,128)(2,1)S(1)}, bf16[64,1024]{1,0:T(8,128)(2,1)S(1)}, f32[256,64,128]{2,1,0:T(8,128)S(1)}, f32[256,64,128]{2,1,0:T(8,128)S(1)}, f32[128,128,128]{2,1,0:T(8,128)S(1)}) custom-call(bf16[64,1024]{1,0:T(8,128)(2,1)} %panel_one.1, bf16[64,1024]{1,0:T(8,128)(2,1)} %panel_two.1, bf16[512,512]{1,0:T(8,128)(2,1)} %inverse_one.1, ...), custom_call_target="tpu_custom_call" | custom-call | tf_op jit(solution)/shard_map/pallas_call | solution.py:597
  67.2 3.0 %shard_map.131 = (bf16[64,1024]{1,0:T(8,128)(2,1)}, bf16[64,1024]{1,0:T(8,128)(2,1)}, bf16[128,128,128]{2,1,0:T(8,128)(2,1)}) custom-call(s32[128]{0:T(128)} %bitcast.7, s32[128]{0:T(128)} %bitcast.8, bf16[64,1024]{1,0:T(8,128)(2,1)S(1)} %get-tuple-element.11.lower_one, bf16[64,1024]{1,0:T(8,128)(2,1)S(1)} %get-tuple-element.12.lower_two, ...), custom_call_target="tpu_custom_call" | custom-call | tf_op jit(solution)/shard_map/pallas_call | solution.py:659
